TPU v7x, 32 devices: a whole 2x2x4 slice. The times are simulated.
32 devices in a mesh: vol: 8 (over z, x), rep: 4 (over y, core).
Axes of the slice: x: 2, y: 2, z: 4, core: 2. Of those that a mesh axis runs over, the one named last changes fastest.
Arguments:
- cutouts: bfloat16 [4, 256, 4096], P('rep', 'vol'), may hold values from -6 to 6
- counts: int32 [4, 8], P('rep', 'vol'), may hold values from 1 to 32, as said below
- partner: int32 [4, 128], P('rep'), may hold values from 0 to 127, as said below
- w_stem: bfloat16 [64, 128], replicated, may hold values from -0.75 to 0.75
- w_mix: bfloat16 [128, 128], replicated, may hold values from -0.5 to 0.5
- w_out: bfloat16 [128, 128], replicated, may hold values from -0.5 to 0.5
- w_proj: bfloat16 [128, 64], replicated, may hold values from -0.5 to 0.5
Outputs:
- upd_stem: float32 [64, 128], replicated
- upd_mix: float32 [128, 128], replicated
- upd_out: float32 [128, 128], replicated
- upd_proj: float32 [128, 64], replicated
- node_loss: float32 [4, 8, 16], P('rep', 'vol')
Inputs may be any that keep to these rules, and one draw needn't show every extreme that they name: `counts`: each row sums to 128, and its largest entry is exactly 32. Each row pairs the nodes of a group: partner[r, partner[r, g]] = g and partner[r, g] != g.
All inputs are finite; a program needn't handle non-finite values.
Results may differ from a plain program's by a relative error of at most 0.0035.
Values may be sent and summed in bfloat16 or wider, within the bound.
No kernel may reach another device: no remote copies, remote signals or barrier semaphores. Data moves between devices by JAX's collectives and lax.ppermute only.
A program may use at most 64 MiB of HBM per device.

v0:
```python
import jax
import jax.numpy as jnp
from jax import lax
from jax.sharding import PartitionSpec as P

logit_divisor_factor = 0.2
norm_eps = 1e-06
rms_eps = 1e-06


def prefix(part, axis, combine, identity):
    place = lax.axis_index(axis)
    gathered = lax.all_gather(part, axis)
    state = jnp.zeros_like(part) + jnp.asarray(identity, part.dtype)

    def one(lap, state):
        return combine(state, lax.dynamic_index_in_dim(gathered, lap, 0, False))

    return lax.fori_loop(0, place, one, state)


def first_dot(left, right):
    return lax.dot_general(
        left, right, (((0,), (0,)), ((), ())), preferred_element_type=jnp.float32
    )


def concluding_matrix_multiply(left, right):
    return lax.dot_general(
        left, right, (((1,), (1,)), ((), ())), preferred_element_type=jnp.float32
    )


def silu_slope(value):
    sigma = jax.nn.sigmoid(value)
    return sigma * (1.0 + value * (1.0 - sigma))


def encode(cutout_rows, w_stem, w_mix, w_out, w_proj):
    number = cutout_rows.shape[0]
    patches = cutout_rows.reshape(-1, w_stem.shape[0])
    per_cutout = patches.shape[0] // number
    pre_stem = jnp.dot(patches, w_stem, preferred_element_type=jnp.float32)
    hidden = jax.nn.silu(pre_stem).astype(jnp.bfloat16)
    pre_mix = jnp.dot(hidden, w_mix, preferred_element_type=jnp.float32)
    mixed = jax.nn.silu(pre_mix).astype(jnp.bfloat16)
    summed = hidden.astype(jnp.float32) + jnp.dot(mixed, w_out, preferred_element_type=jnp.float32)
    pooled = jnp.mean(summed.reshape(number, per_cutout, -1), axis=1).astype(jnp.bfloat16)
    raw_embed = jnp.dot(pooled, w_proj, preferred_element_type=jnp.float32)
    inv_norm = lax.rsqrt(jnp.sum(raw_embed * raw_embed, axis=1, keepdims=True) + norm_eps)
    unit_embed = raw_embed * inv_norm
    return (unit_embed, (patches, pre_stem, hidden, pre_mix, mixed, pooled, unit_embed, inv_norm))


def backward(feature_vector_derivative, saved, w_mix, w_out, w_proj):
    patches, pre_stem, hidden, pre_mix, mixed, pooled, unit_embed, inv_norm = saved
    number = pooled.shape[0]
    per_cutout = patches.shape[0] // number
    channels = hidden.shape[1]
    radial = jnp.sum(unit_embed * feature_vector_derivative, axis=1, keepdims=True)
    grad_raw = (inv_norm * (feature_vector_derivative - unit_embed * radial)).astype(jnp.bfloat16)
    grad_proj = first_dot(pooled, grad_raw)
    grad_pool = (concluding_matrix_multiply(grad_raw, w_proj) / per_cutout).astype(jnp.bfloat16)
    mixed_sum = jnp.sum(mixed.reshape(number, per_cutout, channels), axis=1, dtype=jnp.float32)
    grad_out = lax.dot_general(
        mixed_sum,
        grad_pool.astype(jnp.float32),
        (((0,), (0,)), ((), ())),
        precision=lax.Precision.HIGHEST,
        preferred_element_type=jnp.float32,
    )
    grad_mixed = concluding_matrix_multiply(grad_pool, w_out)
    mix_slope = silu_slope(pre_mix).reshape(number, per_cutout, channels)
    grad_pre_mix = (grad_mixed[:, None, :] * mix_slope).reshape(-1, channels).astype(jnp.bfloat16)
    grad_mix = first_dot(hidden, grad_pre_mix)
    spread_pool = jnp.broadcast_to(
        grad_pool.astype(jnp.float32)[:, None, :], (number, per_cutout, channels)
    ).reshape(-1, channels)
    grad_hidden = spread_pool + concluding_matrix_multiply(grad_pre_mix, w_mix)
    grad_pre_stem = (grad_hidden * silu_slope(pre_stem)).astype(jnp.bfloat16)
    grad_stem = first_dot(patches, grad_pre_stem)
    return (grad_stem, grad_mix, grad_out, grad_proj)


def contrast(anchor_feature_matrix, whole_feature_matrix, self_pos, pair_pos):
    cosine_affinity_matrix = (
        concluding_matrix_multiply(anchor_feature_matrix, whole_feature_matrix)
        / logit_divisor_factor
    )
    columns = lax.broadcasted_iota(jnp.int32, cosine_affinity_matrix.shape, 1)
    exp_scores = jnp.where(columns == self_pos[:, None], 0.0, jnp.exp(cosine_affinity_matrix))
    log_total = jnp.log(jnp.sum(exp_scores, axis=1))
    companion_feature_vector = jnp.take(whole_feature_matrix, pair_pos, axis=0).astype(jnp.float32)
    positive_couple_affinity = (
        jnp.sum(anchor_feature_matrix.astype(jnp.float32) * companion_feature_vector, axis=1)
        / logit_divisor_factor
    )
    return (exp_scores, log_total, companion_feature_vector, log_total - positive_couple_affinity)


def add_counts(earlier, later):
    return earlier + later


def locate(recv_ids, node_rank, slot_index):
    matches = recv_ids[None, :] == node_rank[:, None]
    from_slot = jnp.sum(jnp.where(matches, slot_index[None, :], 0), axis=1)
    return (matches, from_slot)


def on_device(cutouts, counts, partner, w_stem, w_mix, w_out, w_proj):
    vol_size = lax.axis_size("vol")
    vol_index = lax.axis_index("vol")
    max_nodes = cutouts.shape[1]
    node_dev = partner.shape[1] // vol_size
    capacity = (max_nodes + vol_size - 1) // vol_size
    own_cutouts = cutouts[0]
    own_count = counts[0, 0]
    offset = prefix(counts, "vol", add_counts, jnp.zeros_like(counts))[0, 0]
    slot_index = jnp.arange(vol_size * capacity, dtype=jnp.int32)
    target = slot_index // capacity
    first_rank = (offset - target + vol_size - 1) // vol_size
    slot_rank = first_rank + slot_index % capacity
    local_slot = slot_rank * vol_size + target - offset
    is_live = local_slot < own_count
    local_safe = jnp.clip(local_slot, 0, max_nodes - 1)
    send_ids = jnp.where(is_live, slot_rank, -1).astype(jnp.int32)
    node_rank = jnp.arange(node_dev, dtype=jnp.int32)
    packed = jnp.where(
        is_live[:, None], jnp.take(own_cutouts, local_safe, axis=0), jnp.zeros((), jnp.bfloat16)
    )
    arrived, recv_ids = (
        lax.all_to_all(packed, "vol", split_axis=0, concat_axis=0, tiled=True),
        lax.all_to_all(send_ids, "vol", split_axis=0, concat_axis=0, tiled=True),
    )
    matches, from_slot = locate(recv_ids, node_rank, slot_index)
    unit_embed, saved = encode(jnp.take(arrived, from_slot, axis=0), w_stem, w_mix, w_out, w_proj)
    anchor_feature_matrix = unit_embed.astype(jnp.bfloat16)
    whole_feature_matrix = lax.all_gather(anchor_feature_matrix, "vol", axis=0, tiled=True)
    self_pos = vol_index * node_dev + node_rank
    node_global = node_rank * vol_size + vol_index
    pair_global = jnp.take(partner[0], node_global)
    pair_pos = pair_global % vol_size * node_dev + pair_global // vol_size
    exp_scores, log_total, companion_feature_vector, node_loss = contrast(
        anchor_feature_matrix, whole_feature_matrix, self_pos, pair_pos
    )
    row_weight = (exp_scores * jnp.exp(-log_total)[:, None]).astype(jnp.bfloat16)
    horizontal_objective_term = jnp.dot(
        row_weight, whole_feature_matrix, preferred_element_type=jnp.float32
    )
    all_totals = lax.all_gather(log_total, "vol", axis=0, tiled=True)
    column_weight = (exp_scores * jnp.exp(-all_totals)[None, :]).astype(jnp.bfloat16)
    vertical_objective_term = jnp.dot(
        column_weight, whole_feature_matrix, preferred_element_type=jnp.float32
    )
    feature_vector_derivative = (
        horizontal_objective_term + vertical_objective_term - 2.0 * companion_feature_vector
    ) / logit_divisor_factor
    grads = backward(feature_vector_derivative, saved, w_mix, w_out, w_proj)
    grad_totals = lax.psum((grads[0], grads[1], grads[2], grads[3]), ("vol", "rep"))
    updates = [
        summed_grad * lax.rsqrt(jnp.mean(summed_grad * summed_grad) + rms_eps)
        for summed_grad in grad_totals
    ]
    return (updates[0], updates[1], updates[2], updates[3], node_loss[None, None, :])


def solution(mesh):
    in_specs = (P("rep", "vol", None), P("rep", "vol"), P("rep", None), P(), P(), P(), P())
    out_specs = (P(), P(), P(), P(), P("rep", "vol", None))
    return jax.shard_map(
        on_device, mesh=mesh, in_specs=in_specs, out_specs=out_specs, check_vma=False
    )
```

profile of v0, /device:TPU:0, one launch (start us, length us, event | category | flops | bytes accessed | tf_op | source)
XLA Modules:
  0.0 372.9 jit_solution(8634578186639433932)
XLA Ops:
  7.9 0.6 dynamic-slice
  8.5 0.7 bitcast_dynamic-update-slice_fusion
  9.2 13.1 %all-reduce = s32[8]{0:T(128)S(1)} all-reduce(s32[8]{0:T(128)S(1)} %bitcast_dynamic-update-slice_fusion), channel_id=2, replica_groups=mesh['vol'=8,'rep'=4] {'vol'}, use_global_device_ids=true, to_apply=%add | all-reduce | flops 8 | bytes 64
  22.3 0.6 compare_select_fusion
  22.9 11.2 %all-to-all-start = ((s32[8,4,1]{1,2,0:T(1,128)}), s32[8,4,1]{1,2,0:T(1,128)S(1)}, u32[]{:S(2)}, u32[]{:S(2)}) async-start(s32[8,4,1]{1,2,0:T(1,128)} %compare_select_fusion), calls=%async_computation | async-start | bytes 8192 | tf_op jit(solution)/shard_map/all_to_all | solution.py:134
  34.2 0.6 copy-done.1
  34.8 0.7 gather_fusion.2
  35.6 0.7 gather_fusion
  36.5 0.9 select_select_fusion
  38.0 2.5 all-to-all-done
  40.6 3.5 all-to-all-start.1
  44.1 0.5 broadcast.952
  44.6 0.7 reduce.3
  45.7 6.6 %all-to-all-done.1 = bf16[8,4,4096]{2,1,0:T(4,128)(2,1)S(1)} async-done(((bf16[8,4,4096]{2,1,0:T(4,128)(2,1)}), bf16[8,4,4096]{2,1,0:T(4,128)(2,1)S(1)}, u32[]{:S(2)}, u32[]{:S(2)}) %all-to-all-start.1) | async-done | bytes 262176 | tf_op jit(solution)/shard_map/all_to_all | solution.py:133
  52.4 0.6 gather_fusion.1
  53.0 0.2 gather.25
  53.3 0.5 copy-done.9
  53.7 0.9 multiply_convert_fusion.1
  54.7 0.3 convert_reduce_fusion
  55.0 0.4 copy-done.7
  55.4 0.2 bitcast_reduce_fusion
  55.6 0.5 copy-done.6
  56.1 0.2 multiply_reduce_fusion.5
  56.4 30.6 %all_gather.14 = bf16[128,64]{1,0:T(8,128)(2,1)S(1)} all-gather(bf16[16,64]{1,0:T(8,128)(2,1)S(1)} %multiply_convert_fusion.6), channel_id=1, replica_groups=mesh['vol'=8,'rep'=4] {'vol'}, dimensions={0}, use_global_device_ids=true | all-gather | bytes 18432 | tf_op jit(solution)/shard_map/all_gather | solution.py:139
  87.1 0.6 gather_fusion.3
  87.6 0.3 fusion.49
  87.9 0.2 fusion.15
  88.1 0.5 subtract_bitcast_fusion
  88.6 18.7 %all-reduce.1 = f32[128]{0:T(128)S(1)} all-reduce(f32[128]{0:T(128)S(1)} %get-tuple-element.60), channel_id=1, replica_groups=mesh['vol'=8,'rep'=4] {'vol'}, use_global_device_ids=true, to_apply=%add.1 | all-reduce | flops 128 | bytes 1024
  107.3 0.2 fusion.22
  107.5 0.2 multiply_reduce_fusion.4
  108.0 0.8 fusion.31
  108.9 0.2 fusion.8
  109.2 0.9 fusion.51
  110.1 1.1 fusion.2
  111.3 0.9 fusion.52
  112.2 116.4 %all-reduce.7.cloned.1.call-done = (f32[64,128]{1,0:T(8,128)}, f32[128,64]{0,1:T(8,128)}) async-done(((f32[64,128]{1,0:T(8,128)}, f32[128,64]{0,1:T(8,128)}), (f32[64,128]{1,0:T(8,128)}, f32[128,64]{0,1:T(8,128)})) %all-reduce.7.cloned.1.call-update) | async-done | bytes 65552 | tf_op jit(solution)/shard_map/psum | solution.py:160
  228.6 1.4 multiply_reduce_fusion.2
  230.7 0.6 multiply_reduce_fusion.3
  232.0 0.6 broadcast_multiply_fusion.3
  232.6 0.1 copy-done.4
  232.8 0.6 broadcast_multiply_fusion.2
  233.4 127.7 %all-reduce.9.cloned.1.call-done = (f32[128,128]{1,0:T(8,128)}, f32[128,128]{1,0:T(8,128)}) async-done(((f32[128,128]{1,0:T(8,128)}, f32[128,128]{1,0:T(8,128)}), (f32[128,128]{1,0:T(8,128)}, f32[128,128]{1,0:T(8,128)})) %all-reduce.9.cloned.1.call-update) | async-done | bytes 131088 | tf_op jit(solution)/shard_map/psum | solution.py:160
  361.1 1.5 multiply_reduce_fusion
  363.3 0.6 multiply_reduce_fusion.1
  364.6 0.6 broadcast_multiply_fusion.1
  365.2 0.2 copy-done.2
  365.4 0.6 broadcast_multiply_fusion
  (48 shorter events, 1.3 us)
Async XLA Ops:
  7.2 28.5 %copy-start = (bf16[1,32,4096]{2,1,0:T(8,128)(2,1)S(1)}, bf16[1,32,4096]{2,1,0:T(8,128)(2,1)}, u32[]{:S(2)}) copy-start(bf16[1,32,4096]{2,1,0:T(8,128)(2,1)} %param.9) | copy-start | bytes 786436
  7.2 0.7 copy-start.10
  22.9 17.6 %all-to-all-start = ((s32[8,4,1]{1,2,0:T(1,128)}), s32[8,4,1]{1,2,0:T(1,128)S(1)}, u32[]{:S(2)}, u32[]{:S(2)}) async-start(s32[8,4,1]{1,2,0:T(1,128)} %compare_select_fusion), calls=%async_computation | async-start | bytes 8192 | tf_op jit(solution)/shard_map/all_to_all | solution.py:134
  34.2 0.7 copy-start.1
  40.6 11.7 %all-to-all-start.1 = ((bf16[8,4,4096]{2,1,0:T(4,128)(2,1)}), bf16[8,4,4096]{2,1,0:T(4,128)(2,1)S(1)}, u32[]{:S(2)}, u32[]{:S(2)}) async-start(bf16[8,4,4096]{2,1,0:T(4,128)(2,1)} %select_select_fusion), calls=%async_computation.1 | async-start | bytes 524288 | tf_op jit(solution)/shard_map/all_to_all | solution.py:133
  44.1 184.6 %all-reduce.7.cloned.1.call-start = ((), (), s32[]{:S(2)}) async-start(), calls=%async_computation.2 | async-start | bytes 131072 | tf_op jit(solution)/shard_map/psum | solution.py:160
  53.0 0.7 copy-start.9
  53.7 0.9 copy-start.8
  54.6 0.8 copy-start.7
  55.4 0.7 copy-start.6
  111.2 249.8 %all-reduce.9.cloned.1.call-start = ((), (), s32[]{:S(2)}) async-start(), calls=%async_computation.3 | async-start | bytes 262144 | tf_op jit(solution)/shard_map/psum | solution.py:160
  228.6 2.1 copy-start.5
  232.0 0.8 copy-start.4
  361.1 2.2 copy-start.3
  364.6 0.8 copy-start.2
Sparse Core Ops, SparseCore 0:
  111.4 117.2 all-reduce.6
  234.9 126.0 all-reduce.8
where the time goes:
time: 374 us; the launch traced here: 373 us
  waiting for transfers between devices  253 us (68%)
  blocking collectives  62.4 us (17%)
  between operations  18.4 us (5%)
  starting transfers between devices  14.8 us (4%)
  other arithmetic  10.2 us (3%)
  local copies, waits for them, and re-layouts  7.41 us (2%)
  matrix products  6.33 us (2%)
    psum x2, waiting for transfers between devices, on_device(): lax.psum((grads[0], grads[1], grads[2], grads[3]), ('vol', 'rep'))  244 us
    unnamed x2, blocking collectives  31.8 us
    all_gather x1, blocking collectives, on_device(): lax.all_gather(anchor_feature_matrix, 'vol', axis=0, tiled=True)  30.6 us
    all_to_all x1, starting transfers between devices, on_device(): lax.all_to_all(send_ids, 'vol', split_axis=0, concat_axis=0, tiled=True)  11.2 us
  transfers between devices with their start and end apart: 4, of which 4 were waited for; matrix products, arithmetic and copies ran while one was open for 2% of the time, Pallas kernels for 0%

commit v1 on v0

--- a/solution.py
+++ b/solution.py
@@ -157,7 +157,7 @@
         horizontal_objective_term + vertical_objective_term - 2.0 * companion_feature_vector
     ) / logit_divisor_factor
     grads = backward(feature_vector_derivative, saved, w_mix, w_out, w_proj)
-    grad_totals = lax.psum((grads[0], grads[1], grads[2], grads[3]), ("vol", "rep"))
+    grad_totals = lax.psum(lax.psum((grads[0], grads[1], grads[2], grads[3]), "rep"), "vol")
     updates = [
         summed_grad * lax.rsqrt(jnp.mean(summed_grad * summed_grad) + rms_eps)
         for summed_grad in grad_totals

time: 374 us -> 334 us (0.89)
  waiting for transfers between devices: 253 us -> 214 us
    psum x2 -> x4, waiting for transfers between devices: 244 us -> 205 us  [the longest x2 142 us: on_device(): lax.psum(lax.psum((grads[0], grads[1], grads[2], grads[3]), 'rep'), 'vol')]
  transfers between devices with their start and end apart: 4 -> 6, of which waited for: 4 -> 6; matrix products, arithmetic and copies ran while one was open for 2% -> 2% of each run, Pallas kernels for 0% -> 0%
where the time goes in v1:
time: 334 us
  waiting for transfers between devices  214 us (64%)
  blocking collectives  62.4 us (19%)
  between operations  18.2 us (5%)
  starting transfers between devices  14.9 us (4%)
  other arithmetic  10.2 us (3%)
  local copies, waits for them, and re-layouts  7.41 us (2%)
  matrix products  6.33 us (2%)
    psum x2, waiting for transfers between devices, on_device(): lax.psum(lax.psum((grads[0], grads[1], grads[2], grads[3]), 'rep'), 'vol')  142 us
    psum x2, waiting for transfers between devices, on_device(): lax.psum((grads[0], grads[1], grads[2], grads[3]), 'rep')  62.7 us
    unnamed x2, blocking collectives  31.8 us
    all_gather x1, blocking collectives, on_device(): lax.all_gather(anchor_feature_matrix, 'vol', axis=0, tiled=True)  30.6 us
    all_to_all x1, starting transfers between devices, on_device(): lax.all_to_all(send_ids, 'vol', split_axis=0, concat_axis=0, tiled=True)  11.2 us
  transfers between devices with their start and end apart: 6, of which 6 were waited for; matrix products, arithmetic and copies ran while one was open for 2% of the time, Pallas kernels for 0%

profile of v1, /device:TPU:0, one launch (start us, length us, event | category | flops | bytes accessed | tf_op | source)
XLA Modules:
  0.0 333.7 jit_solution(293185939644723265)
XLA Ops:
  7.9 0.6 dynamic-slice
  8.5 0.7 bitcast_dynamic-update-slice_fusion
  9.2 13.1 %all-reduce = s32[8]{0:T(128)S(1)} all-reduce(s32[8]{0:T(128)S(1)} %bitcast_dynamic-update-slice_fusion), channel_id=2, replica_groups=mesh['vol'=8,'rep'=4] {'vol'}, use_global_device_ids=true, to_apply=%add | all-reduce | flops 8 | bytes 64
  22.3 0.6 compare_select_fusion
  22.9 11.2 %all-to-all-start = ((s32[8,4,1]{1,2,0:T(1,128)}), s32[8,4,1]{1,2,0:T(1,128)S(1)}, u32[]{:S(2)}, u32[]{:S(2)}) async-start(s32[8,4,1]{1,2,0:T(1,128)} %compare_select_fusion), calls=%async_computation | async-start | bytes 8192 | tf_op jit(solution)/shard_map/all_to_all | solution.py:134
  34.2 0.6 copy-done.1
  34.8 0.7 gather_fusion.2
  35.6 0.7 gather_fusion
  36.5 0.9 select_select_fusion
  38.0 2.5 all-to-all-done
  40.6 3.5 %all-to-all-start.1 = ((bf16[8,4,4096]{2,1,0:T(4,128)(2,1)}), bf16[8,4,4096]{2,1,0:T(4,128)(2,1)S(1)}, u32[]{:S(2)}, u32[]{:S(2)}) async-start(bf16[8,4,4096]{2,1,0:T(4,128)(2,1)} %select_select_fusion), calls=%async_computation.1 | async-start | bytes 524288 | tf_op jit(solution)/shard_map/all_to_all | solution.py:133
  44.1 0.5 broadcast.952
  44.6 0.7 reduce.3
  45.7 6.6 %all-to-all-done.1 = bf16[8,4,4096]{2,1,0:T(4,128)(2,1)S(1)} async-done(((bf16[8,4,4096]{2,1,0:T(4,128)(2,1)}), bf16[8,4,4096]{2,1,0:T(4,128)(2,1)S(1)}, u32[]{:S(2)}, u32[]{:S(2)}) %all-to-all-start.1) | async-done | bytes 262176 | tf_op jit(solution)/shard_map/all_to_all | solution.py:133
  52.4 0.6 gather_fusion.1
  53.0 0.2 gather.25
  53.3 0.5 copy-done.9
  53.7 0.9 multiply_convert_fusion.1
  54.7 0.3 convert_reduce_fusion
  55.0 0.4 copy-done.7
  55.4 0.2 bitcast_reduce_fusion
  55.6 0.5 copy-done.6
  56.1 0.2 multiply_reduce_fusion.5
  56.4 30.6 %all_gather.14 = bf16[128,64]{1,0:T(8,128)(2,1)S(1)} all-gather(bf16[16,64]{1,0:T(8,128)(2,1)S(1)} %multiply_convert_fusion.6), channel_id=1, replica_groups=mesh['vol'=8,'rep'=4] {'vol'}, dimensions={0}, use_global_device_ids=true | all-gather | bytes 18432 | tf_op jit(solution)/shard_map/all_gather | solution.py:139
  87.1 0.6 gather_fusion.3
  87.6 0.3 fusion.49
  87.9 0.2 fusion.15
  88.1 0.5 subtract_bitcast_fusion
  88.6 18.7 %all-reduce.1 = f32[128]{0:T(128)S(1)} all-reduce(f32[128]{0:T(128)S(1)} %get-tuple-element.64), channel_id=1, replica_groups=mesh['vol'=8,'rep'=4] {'vol'}, use_global_device_ids=true, to_apply=%add.1 | all-reduce | flops 128 | bytes 1024
  107.5 0.2 multiply_reduce_fusion.4
  108.0 0.8 fusion.31
  108.9 0.2 fusion.8
  109.2 0.9 fusion.51
  110.1 1.1 fusion.2
  111.3 0.9 fusion.52
  112.2 28.0 %all-reduce.15.cloned.1.call-done = (f32[64,128]{1,0:T(8,128)}, f32[128,64]{0,1:T(8,128)}) async-done(((f32[64,128]{1,0:T(8,128)}, f32[128,64]{0,1:T(8,128)}), (f32[64,128]{1,0:T(8,128)}, f32[128,64]{0,1:T(8,128)})) %all-reduce.15.cloned.1.call-update) | async-done | bytes 65552 | tf_op jit(solution)/shard_map/psum | solution.py:160
  140.3 34.7 %all-reduce.17.cloned.1.call-done = (f32[128,128]{1,0:T(8,128)}, f32[128,128]{1,0:T(8,128)}) async-done(((f32[128,128]{1,0:T(8,128)}, f32[128,128]{1,0:T(8,128)}), (f32[128,128]{1,0:T(8,128)}, f32[128,128]{1,0:T(8,128)})) %all-reduce.17.cloned.1.call-update) | async-done | bytes 131088 | tf_op jit(solution)/shard_map/psum | solution.py:160
  175.1 73.0 %all-reduce.11.cloned.1.call-done = (f32[64,128]{1,0:T(8,128)}, f32[128,64]{0,1:T(8,128)}) async-done(((f32[64,128]{1,0:T(8,128)}, f32[128,64]{0,1:T(8,128)}), (f32[64,128]{1,0:T(8,128)}, f32[128,64]{0,1:T(8,128)})) %all-reduce.11.cloned.1.call-update) | async-done | bytes 65552 | tf_op jit(solution)/shard_map/psum | solution.py:160
  248.1 1.4 multiply_reduce_fusion.2
  250.2 0.6 multiply_reduce_fusion.3
  251.5 0.6 broadcast_multiply_fusion.3
  252.3 0.6 broadcast_multiply_fusion.2
  252.9 69.3 %all-reduce.13.cloned.1.call-done = (f32[128,128]{1,0:T(8,128)}, f32[128,128]{1,0:T(8,128)}) async-done(((f32[128,128]{1,0:T(8,128)}, f32[128,128]{1,0:T(8,128)}), (f32[128,128]{1,0:T(8,128)}, f32[128,128]{1,0:T(8,128)})) %all-reduce.13.cloned.1.call-update) | async-done | bytes 131088 | tf_op jit(solution)/shard_map/psum | solution.py:160
  322.1 1.5 multiply_reduce_fusion
  324.3 0.6 multiply_reduce_fusion.1
  325.7 0.6 broadcast_multiply_fusion.1
  326.3 0.2 copy-done.2
  326.5 0.6 broadcast_multiply_fusion
  (54 shorter events, 1.7 us)
Async XLA Ops:
  7.2 28.5 %copy-start = (bf16[1,32,4096]{2,1,0:T(8,128)(2,1)S(1)}, bf16[1,32,4096]{2,1,0:T(8,128)(2,1)}, u32[]{:S(2)}) copy-start(bf16[1,32,4096]{2,1,0:T(8,128)(2,1)} %param.9) | copy-start | bytes 786436
  7.2 0.7 copy-start.10
  22.9 17.6 %all-to-all-start = ((s32[8,4,1]{1,2,0:T(1,128)}), s32[8,4,1]{1,2,0:T(1,128)S(1)}, u32[]{:S(2)}, u32[]{:S(2)}) async-start(s32[8,4,1]{1,2,0:T(1,128)} %compare_select_fusion), calls=%async_computation | async-start | bytes 8192 | tf_op jit(solution)/shard_map/all_to_all | solution.py:134
  34.2 0.7 copy-start.1
  40.6 11.7 %all-to-all-start.1 = ((bf16[8,4,4096]{2,1,0:T(4,128)(2,1)}), bf16[8,4,4096]{2,1,0:T(4,128)(2,1)S(1)}, u32[]{:S(2)}, u32[]{:S(2)}) async-start(bf16[8,4,4096]{2,1,0:T(4,128)(2,1)} %select_select_fusion), calls=%async_computation.1 | async-start | bytes 524288 | tf_op jit(solution)/shard_map/all_to_all | solution.py:133
  44.1 96.2 %all-reduce.15.cloned.1.call-start = ((), (), s32[]{:S(2)}) async-start(), calls=%async_computation.4 | async-start | bytes 131072 | tf_op jit(solution)/shard_map/psum | solution.py:160
  53.0 0.7 copy-start.9
  53.7 0.9 copy-start.8
  54.6 0.8 copy-start.7
  55.4 0.7 copy-start.6
  111.2 63.8 %all-reduce.17.cloned.1.call-start = ((), (), s32[]{:S(2)}) async-start(), calls=%async_computation.5 | async-start | bytes 262144 | tf_op jit(solution)/shard_map/psum | solution.py:160
  112.2 135.9 %all-reduce.11.cloned.1.call-start = ((), (), s32[]{:S(2)}) async-start(), calls=%async_computation.2 | async-start | bytes 131072 | tf_op jit(solution)/shard_map/psum | solution.py:160
  140.3 181.9 %all-reduce.13.cloned.1.call-start = ((), (), s32[]{:S(2)}) async-start(), calls=%async_computation.3 | async-start | bytes 262144 | tf_op jit(solution)/shard_map/psum | solution.py:160
  248.1 2.1 copy-start.5
  251.5 0.8 copy-start.4
  322.1 2.2 copy-start.3
  325.6 0.8 copy-start.2
Sparse Core Ops, SparseCore 0:
  111.4 28.8 all-reduce.14
  143.2 31.7 all-reduce.16
  178.6 69.4 all-reduce.10
  251.4 70.6 all-reduce.12
